TPU v7x, 32 devices: a whole 2x2x4 slice. The times are simulated.
32 devices in a mesh: clus: 4 (over y, x), trip: 4 (over z), mode: 2 (over core).
Axes of the slice: x: 2, y: 2, z: 4, core: 2. Of those that a mesh axis runs over, the one named last changes fastest.
Arguments:
- force_third: bfloat16 [8, 90, 8100], P('clus', 'mode'), may hold values from -0.0234375 to 0.0234375
- phase_angle: bfloat16 [8, 16], P('clus', 'trip'), may hold values from -3.140625 to 3.140625
- eigenvectors: bfloat16 [32, 90, 180], P('trip'), may hold values from -0.4375 to 0.4375
- frequencies: bfloat16 [32, 90], P('trip'), may hold values from 0.5 to 2
- deviation: bfloat16 [32, 90], P('trip'), may hold values from 0.5 to 2
- send_rows: int32 [4, 32], P('trip'), may hold values from 0 to 7
- trip_table: int32 [16, 3], P('trip'), may hold values from 0 to 31
- irreducible: int32 [16], P('trip'), may hold values from 0 to 3
- multiplicity: int32 [16], P('trip'), may hold values from 1 to 8
- drive_term: float32 [4, 90], P('trip', 'mode'), may hold values from -120 to 120
- boundary: float32 [4, 90], P('trip', 'mode'), may hold values from 5 to 40
Outputs:
- gamma_total: float32 [4, 90], P('trip', 'mode')
- new_deviation: float32 [4, 90], P('trip', 'mode')
All inputs are finite; a program needn't handle non-finite values.
Results may differ from a plain program's by a relative error of at most 0.00095.
Values may be sent and summed in bfloat16 or wider, within the bound.
A program may use at most 64 MiB of HBM per device.

v0:
```python
import functools

import jax
import jax.numpy as jnp
from jax import lax
from jax.experimental import pallas as pl
from jax.experimental.pallas import tpu as pltpu
from jax.sharding import PartitionSpec as P

smearing = 0.3
MESH = pl.DeviceIdType.MESH
LANES = 128
f32 = jnp.float32
bf16 = jnp.bfloat16


def up(value, step):
    return -(-value // step) * step


def pick(index, options):
    chosen = options[0]
    for position in range(1, len(options)):
        chosen = jnp.where(index == position, options[position], chosen)
    return chosen


def kernel(
    dims,
    force_ref,
    eig_ref,
    send_rows_ref,
    table_ref,
    irr_ref,
    mult_ref,
    drive_ref,
    bound_ref,
    gamma_ref,
    dev_ref,
    blocks,
    outgoing,
    arrived,
    mine,
    other,
    zbuf,
    tre,
    tim,
    w0buf,
    ratebuf,
    coupbuf,
    msg,
    inbox,
    f_send,
    f_recv,
    e_send,
    e_recv,
    p_send,
    p_recv,
    m_send,
    m_recv,
):
    n_clus, n_trip, n_mode, modes, half, rp, cl, slot, chunk = dims
    ep = eig_ref.shape[1]
    npad = force_ref.shape[1]
    me_c = lax.axis_index("clus")
    me_t = lax.axis_index("trip")
    me_m = lax.axis_index("mode")
    sib = (me_c, me_t, 1 - me_m)

    peers = []
    for dt in range(n_trip):
        for dc in range(n_clus):
            if dt or dc:
                peers.append((dt, dc))

    def peer_id(dt, dc):
        return (lax.rem(me_c + dc, n_clus), lax.rem(me_t + dt, n_trip), me_m)

    barrier = pltpu.get_barrier_semaphore()
    for dt, dc in peers:
        pl.semaphore_signal(barrier, inc=1, device_id=peer_id(dt, dc), device_id_type=MESH)
    pl.semaphore_signal(barrier, inc=1, device_id=sib, device_id_type=MESH)

    for dt in range(n_trip):
        target = lax.rem(me_t + dt, n_trip)
        for j in range(slot):
            row = send_rows_ref[0, target * slot + j]
            outgoing[dt, j] = eig_ref[row]

    pl.semaphore_wait(barrier, len(peers) + 1)

    def xor_id(k):
        low, high = lax.rem(me_c, 2), me_c // 2
        if k & 1:
            low = 1 - low
        if k & 2:
            high = 1 - high
        return (high * 2 + low, me_t, me_m)

    def unit(k, m, r):
        return blocks.at[k, m, pl.ds(r * rp, rp)]

    started = []

    def send(src, dst, k, m, r, device):
        copy = pltpu.make_async_remote_copy(
            src_ref=src,
            dst_ref=dst,
            send_sem=f_send.at[k, m, r],
            recv_sem=f_recv.at[k, m, r],
            device_id=device,
            device_id_type=MESH,
        )
        copy.start()
        started.append(copy)

    def got(k, m, r):
        pltpu.make_async_remote_copy(
            src_ref=unit(k, m, r),
            dst_ref=unit(k, m, r),
            send_sem=f_send.at[k, m, r],
            recv_sem=f_recv.at[k, m, r],
            device_id=sib,
            device_id_type=MESH,
        ).wait_recv()

    def own(r):
        return force_ref.at[pl.ds(r * rp, rp)]

    send(own(0), unit(1, 0, 0), 1, 0, 0, xor_id(1))
    send(own(1), unit(2, 0, 1), 2, 0, 1, xor_id(2))
    send(own(1), unit(1, 0, 1), 1, 0, 1, xor_id(1))
    send(own(0), unit(2, 0, 0), 2, 0, 0, xor_id(2))
    for r in range(cl):
        send(own(r), unit(0, 1, r), 0, 1, r, sib)

    eig_copies = []
    for dt in range(1, n_trip):
        copy = pltpu.make_async_remote_copy(
            src_ref=outgoing.at[dt],
            dst_ref=arrived.at[dt],
            send_sem=e_send.at[dt],
            recv_sem=e_recv.at[dt],
            device_id=(me_c, lax.rem(me_t + dt, n_trip), me_m),
            device_id_type=MESH,
        )
        copy.start()
        eig_copies.append(copy)
    arrived[0] = outgoing[0]

    got(1, 0, 0)
    send(unit(1, 0, 0), unit(3, 0, 0), 3, 0, 0, xor_id(2))
    send(unit(1, 0, 0), unit(1, 1, 0), 1, 1, 0, sib)
    got(2, 0, 1)
    send(unit(2, 0, 1), unit(3, 0, 1), 3, 0, 1, xor_id(1))
    send(unit(2, 0, 1), unit(2, 1, 1), 2, 1, 1, sib)

    for copy in eig_copies:
        copy.wait()
    for j in range(3):
        entry = table_ref[me_c, j]
        source = entry // slot
        within = entry - source * slot
        offset = lax.rem(me_t - source + n_trip, n_trip)
        mine[j] = arrived[offset * 1, within]
    pair = pltpu.make_async_remote_copy(
        src_ref=mine,
        dst_ref=other,
        send_sem=p_send,
        recv_sem=p_recv,
        device_id=sib,
        device_id_type=MESH,
    )
    pair.start()
    pair.wait()

    first = me_m == 0

    def complex_of(j):
        a = mine[j].astype(f32)
        b = other[j].astype(f32)
        return jnp.where(first, a, b), jnp.where(first, b, a)

    re0, im0 = complex_of(0)
    re1, im1 = complex_of(1)
    re2, im2 = complex_of(2)
    f0 = re0[modes : modes + 1]
    f1, d1 = re1[modes : modes + 1], im1[modes : modes + 1]
    f2, d2 = re2[modes : modes + 1], im2[modes : modes + 1]

    def half_rows(mat):
        return pick(me_m, [mat[m * half : m * half + rp] for m in range(n_mode)])

    fill = jnp.zeros((rp - half, LANES), f32)

    def lead(mat, m):
        part = mat[m * half : (m + 1) * half]
        stacked = jnp.concatenate([part, fill] * cl, axis=0)
        return half_rows(jnp.transpose(stacked))

    lead_re = [lead(re0, m) for m in range(n_mode)]
    lead_im = [lead(im0, m) for m in range(n_mode)]
    lane_k = lax.broadcasted_iota(jnp.int32, (rp, cl * rp), 1)
    lane = lax.broadcasted_iota(jnp.int32, (1, LANES), 1)

    def weights(block_ref, m_rel):
        cosines, sines = [], []
        for r in range(cl):
            tail = block_ref[pl.ds(r * rp + rp - 16, 16), pl.ds(0, LANES)].astype(f32)
            at = 16 - (rp - half)
            cosines.append(jnp.sum(jnp.where(lane == me_c, tail[at : at + 1], 0.0), axis=1, keepdims=True))
            sines.append(jnp.sum(jnp.where(lane == me_c, tail[at + 1 : at + 2], 0.0), axis=1, keepdims=True))
        cosv, sinv = cosines[0], sines[0]
        for r in range(1, cl):
            cosv = jnp.where(lane_k >= r * rp, cosines[r], cosv)
            sinv = jnp.where(lane_k >= r * rp, sines[r], sinv)
        if m_rel == 0:
            wre = jnp.where(first, lead_re[0], lead_re[1])
            wim = jnp.where(first, lead_im[0], lead_im[1])
        else:
            wre = jnp.where(first, lead_re[1], lead_re[0])
            wim = jnp.where(first, lead_im[1], lead_im[0])
        return jnp.concatenate(
            [cosv * wre - sinv * wim, cosv * wim + sinv * wre], axis=0
        ).astype(bf16)

    def accumulate(refs, fresh):
        mats = [weights(ref, m_rel) for ref, m_rel in refs]

        def step(n, carry):
            cols = pl.ds(pl.multiple_of(n * chunk, chunk), chunk)
            total = None
            for mat, (ref, _) in zip(mats, refs):
                part = jnp.dot(mat, ref[:, cols], preferred_element_type=f32)
                total = part if total is None else total + part
            if not fresh:
                total = total + zbuf[:, cols]
            zbuf[:, cols] = total
            return carry

        lax.fori_loop(0, npad // chunk, step, 0)

    e2a = jnp.concatenate([re2, im2], axis=1)[:modes].astype(bf16)
    e2b = jnp.concatenate([-im2, re2], axis=1)[:modes].astype(bf16)
    row_id = lax.broadcasted_iota(jnp.int32, (ep, LANES), 0)
    e1re_t = jnp.transpose(jnp.where(row_id < modes, re1, 0.0))[:ep]
    e1im_t = jnp.transpose(jnp.where(row_id < modes, im1, 0.0))[:ep]
    left_a = jnp.concatenate([e1re_t, e1im_t], axis=0).astype(bf16)
    left_b = jnp.concatenate([-e1im_t, e1re_t], axis=0).astype(bf16)

    def column(row):
        return jnp.transpose(jnp.broadcast_to(row, (LANES, LANES)))

    w0buf[...] = half_rows(jnp.where(row_id.shape[0] > 0, column(f0), 1.0))
    w1 = jnp.where(row_id < modes, column(f1)[:ep], 1.0)
    w2 = jnp.where(lane < modes, f2, 1.0)
    occ = jnp.where(row_id < modes, column(d1)[:ep], 0.0) + jnp.where(lane < modes, d2, 0.0)
    inverse = 1.0 / (w1 * w2)

    for r in range(cl):
        got(0, 1, r)
    accumulate([(force_ref, 0), (blocks.at[0, 1], 1)], True)
    got(1, 0, 1)
    send(unit(1, 0, 1), unit(1, 1, 1), 1, 1, 1, sib)
    got(2, 0, 0)
    send(unit(2, 0, 0), unit(2, 1, 0), 2, 1, 0, sib)
    for k in (1, 2):
        for r in range(cl):
            got(k, 1, r)
    accumulate([(blocks.at[k, m], m) for k in (1, 2) for m in (0, 1)], False)
    got(3, 0, 0)
    send(unit(3, 0, 0), unit(3, 1, 0), 3, 1, 0, sib)
    got(3, 0, 1)
    send(unit(3, 0, 1), unit(3, 1, 1), 3, 1, 1, sib)
    got(3, 1, 0)
    got(3, 1, 1)
    accumulate([(blocks.at[3, 0], 0), (blocks.at[3, 1], 1)], False)

    for b in range(modes):
        part = zbuf[:, b * modes : (b + 1) * modes].astype(bf16)
        out = jnp.dot(part[:rp], e2a, preferred_element_type=f32) + jnp.dot(
            part[rp:], e2b, preferred_element_type=f32
        )
        tre[b * rp : (b + 1) * rp, :] = out[:, :LANES]
        tim[b * rp : (b + 1) * rp, :] = out[:, LANES:]
    tre[modes * rp :, :] = jnp.zeros(((ep - modes) * rp, LANES), f32)
    tim[modes * rp :, :] = jnp.zeros(((ep - modes) * rp, LANES), f32)

    scaled = 0.5 / (smearing * smearing)
    ratebuf[...] = jnp.zeros_like(ratebuf)
    coupbuf[...] = jnp.zeros_like(coupbuf)

    def modes_step(p, carry):
        def rows(ref):
            return jnp.concatenate(
                [ref[pl.ds(2 * p + i, ep, stride=rp), :] for i in range(2)], axis=1
            ).astype(bf16)

        amp = jnp.dot(left_a, rows(tre), preferred_element_type=f32) + jnp.dot(
            left_b, rows(tim), preferred_element_type=f32
        )
        square = amp * amp
        square = square[:ep] + square[ep:]
        for i in range(2):
            w0 = w0buf[pl.ds(2 * p + i, 1), :]
            decays = w0 - w1 - w2
            merges = w0 + w1 - w2
            gauss = jnp.exp(-scaled * decays * decays) + jnp.exp(-scaled * merges * merges)
            value = square[:, i * LANES : (i + 1) * LANES] * gauss * inverse
            ratebuf[pl.ds(2 * p + i, 1), :] = jnp.sum(value, axis=0, keepdims=True)
            coupbuf[pl.ds(2 * p + i, 1), :] = jnp.sum(value * occ, axis=0, keepdims=True)
        return carry

    lax.fori_loop(0, rp // 2, modes_step, 0)

    factor = mult_ref[me_c].astype(f32)
    w0_row = pick(me_m, [f0[:, m * half : (m + 1) * half] for m in range(n_mode)])
    rate = jnp.sum(jnp.transpose(ratebuf[...]), axis=0, keepdims=True)[:, :half] / w0_row * factor
    coup = jnp.sum(jnp.transpose(coupbuf[...]), axis=0, keepdims=True)[:, :half] / w0_row * factor
    msg[...] = jnp.zeros_like(msg)
    msg[0:1, 0:half] = rate
    msg[1:2, 0:half] = coup
    msg[2:3, :] = jnp.full((1, LANES), irr_ref[me_c].astype(f32))

    copies = []
    for index, (dt, dc) in enumerate(peers):
        copy = pltpu.make_async_remote_copy(
            src_ref=msg,
            dst_ref=inbox.at[index],
            send_sem=m_send.at[index],
            recv_sem=m_recv.at[index],
            device_id=peer_id(dt, dc),
            device_id_type=MESH,
        )
        copy.start()
        copies.append(copy)
    for copy in started:
        copy.wait_send()
    for copy in copies:
        copy.wait()

    nq = gamma_ref.shape[0]
    for q in range(nq):
        name = (me_t * nq + q).astype(f32)

        def kept(tile):
            return jnp.where(tile[2:3, :half] == name, tile[0:2, :half], 0.0)

        total = kept(msg[...])
        if len(peers) <= 16:
            for index in range(len(peers)):
                total = total + kept(inbox[index])
        else:
            total = lax.fori_loop(0, len(peers), lambda i, acc: acc + kept(inbox[i]), total)
        gamma = total[0:1] + bound_ref[q : q + 1, :]
        gamma_ref[q : q + 1, :] = gamma
        dev_ref[q : q + 1, :] = (drive_ref[q : q + 1, :] + total[1:2]) / gamma


def body(
    force_third,
    phase_angle,
    eigenvectors,
    frequencies,
    deviation,
    send_rows,
    trip_table,
    irreducible,
    multiplicity,
    drive_term,
    boundary,
):
    n_clus, n_trip, n_mode = (lax.axis_size(name) for name in ("clus", "trip", "mode"))
    cl, half, flat = force_third.shape
    points, modes, _ = eigenvectors.shape
    slot = send_rows.shape[1] // n_trip
    chunk = 512
    rp = up(half + 2, 16)
    ep = up(modes + 1, 16)
    npad = up(flat, chunk)
    angles = phase_angle.astype(f32)
    trig = jnp.stack([jnp.cos(angles), jnp.sin(angles)], axis=1).astype(bf16)
    tail = jnp.pad(trig, ((0, 0), (0, rp - half - 2), (0, npad - trig.shape[2])))
    force = jnp.concatenate(
        [jnp.pad(force_third, ((0, 0), (0, 0), (0, npad - flat))), tail], axis=1
    ).reshape(cl * rp, npad)
    first = lax.axis_index("mode") == 0
    part = jnp.where(first, eigenvectors[..., :modes], eigenvectors[..., modes:])
    extra = jnp.where(first, frequencies, deviation)[:, None]
    eig = jnp.pad(
        jnp.concatenate([part, extra], axis=1),
        ((0, 0), (0, ep - modes - 1), (0, LANES - modes)),
    )
    n_peers = n_clus * n_trip - 1
    vmem = pl.BlockSpec(memory_space=pltpu.VMEM)
    smem = pl.BlockSpec(memory_space=pltpu.SMEM)
    out = jax.ShapeDtypeStruct(boundary.shape, f32)
    dma = pltpu.SemaphoreType.DMA
    return tuple(
        pl.pallas_call(
            functools.partial(
                kernel, (n_clus, n_trip, n_mode, modes, half, rp, cl, slot, chunk)
            ),
            out_shape=(out, out),
            in_specs=[vmem, vmem, smem, smem, smem, smem, vmem, vmem],
            out_specs=(vmem, vmem),
            scratch_shapes=[
                pltpu.VMEM((n_clus, n_mode, cl * rp, npad), bf16),
                pltpu.VMEM((n_trip, slot, ep, LANES), bf16),
                pltpu.VMEM((n_trip, slot, ep, LANES), bf16),
                pltpu.VMEM((3, ep, LANES), bf16),
                pltpu.VMEM((3, ep, LANES), bf16),
                pltpu.VMEM((2 * rp, npad), f32),
                pltpu.VMEM((ep * rp, LANES), f32),
                pltpu.VMEM((ep * rp, LANES), f32),
                pltpu.VMEM((rp, LANES), f32),
                pltpu.VMEM((LANES, LANES), f32),
                pltpu.VMEM((LANES, LANES), f32),
                pltpu.VMEM((8, LANES), f32),
                pltpu.VMEM((n_peers, 8, LANES), f32),
                dma((n_clus, n_mode, cl)),
                dma((n_clus, n_mode, cl)),
                dma((n_trip,)),
                dma((n_trip,)),
                dma,
                dma,
                dma((n_peers,)),
                dma((n_peers,)),
            ],
            compiler_params=pltpu.CompilerParams(
                collective_id=0, has_side_effects=True, vmem_limit_bytes=48 * 1024 * 1024
            ),
        )(force, eig, send_rows, trip_table, irreducible, multiplicity, drive_term, boundary)
    )


def solution(mesh):
    return jax.shard_map(
        body,
        mesh=mesh,
        in_specs=(
            P("clus", "mode", None),
            P("clus", "trip"),
            P("trip", None, None),
            P("trip", None),
            P("trip", None),
            P("trip", None),
            P("trip", None),
            P("trip"),
            P("trip"),
            P("trip", "mode"),
            P("trip", "mode"),
        ),
        out_specs=(P("trip", "mode"), P("trip", "mode")),
        check_vma=False,
    )
```

profile of v0, /device:TPU:0, one launch (start us, length us, event | category | flops | bytes accessed | tf_op | source)
XLA Modules:
  0.0 85.5 jit_solution(17321492786944866593)
XLA Ops:
  0.6 0.7 fusion.15
  1.3 0.1 fusion.10
  1.4 5.5 %fusion = bf16[2,48,8192]{2,0,1:T(2,128)(2,1)S(1)} fusion(bf16[2,45,8100]{2,0,1:T(2,128)(2,1)} %param.11, bf16[2,3,8192]{2,0,1:T(2,128)(2,1)S(1)} %fusion.10), kind=kLoop, calls=%fused_computation.1 | loop fusion | flops 4718592 | bytes 3129168 | tf_op jit(solution)/shard_map/concatenate | solution.py:384
  6.9 0.0 copy-start.7
  6.9 0.0 copy-start.8
  6.9 0.0 copy-start.6
  6.9 0.9 %copy.16 = bf16[2,48,8192]{2,1,0:T(8,128)(2,1)S(1)} copy(bf16[2,48,8192]{2,0,1:T(2,128)(2,1)S(1)} %fusion) | data formatting | bytes 3145728 | tf_op jit(solution)/shard_map/concatenate | solution.py:384
  7.8 0.0 copy-start
  7.8 0.0 copy-start.1
  7.8 0.0 copy-start.2
  7.8 0.0 copy-start.3
  7.8 0.0 copy-start.4
  7.8 0.0 copy-start.5
  7.8 0.0 copy-done.7
  7.9 0.0 copy-done.8
  7.9 0.0 copy-done.6
  7.9 0.1 fusion.16
  8.0 0.1 copy_select_fusion
  8.1 0.1 fusion.6.eig_ref
  8.2 0.3 copy-done
  8.5 0.0 copy-done.1
  8.5 0.0 copy-done.2
  8.5 0.0 copy-done.3
  8.5 0.0 copy-done.4
  8.5 0.0 copy-done.5
  8.5 76.0 %shard_map.122 = (f32[1,45]{1,0:T(1,128)S(1)}, f32[1,45]{1,0:T(1,128)S(1)}) custom-call(bf16[96,8192]{1,0:T(8,128)(2,1)S(1)} %bitcast.7, bf16[8,96,128]{2,1,0:T(8,128)(2,1)S(1)} %fusion.6.eig_ref, s32[1,32]{1,0:T(1,128)S(1)} %copy-done.1, s32[4,3]{1,0:T(4,128)S(1)} %copy-done, s32[4]{0:T(128)S(1)} %copy-done.2, s32[4]{0:T(128)S(1)} %copy-done.3, ...), custom_call_target="tpu_custom_call" | custom-call | tf_op jit(solution)/shard_map/pallas_call | solution.py:400
  84.5 0.5 copy.26
  85.0 0.5 copy.27
  (2 shorter events, 0.0 us)
Async XLA Ops:
  6.9 1.0 %copy-start.7 = (bf16[8,90]{1,0:T(8,128)(2,1)S(1)}, bf16[8,90]{1,0:T(8,128)(2,1)}, u32[]{:S(2)}) copy-start(bf16[8,90]{1,0:T(8,128)(2,1)} %param.14) | copy-start | bytes 4324
  6.9 1.0 %copy-start.8 = (bf16[8,90]{1,0:T(8,128)(2,1)S(1)}, bf16[8,90]{1,0:T(8,128)(2,1)}, u32[]{:S(2)}) copy-start(bf16[8,90]{1,0:T(8,128)(2,1)} %param.15) | copy-start | bytes 4324
  6.9 1.0 %copy-start.6 = (bf16[8,90,180]{2,0,1:T(8,128)(2,1)S(1)}, bf16[8,90,180]{2,0,1:T(8,128)(2,1)}, u32[]{:S(2)}) copy-start(bf16[8,90,180]{2,0,1:T(8,128)(2,1)} %param.13) | copy-start | bytes 777604
  7.8 0.7 copy-start
  7.8 0.7 copy-start.1
  7.8 0.7 copy-start.2
  7.8 0.7 copy-start.3
  7.8 0.7 copy-start.4
  7.8 0.7 copy-start.5
where the time goes:
time: 85.8 us; the launch traced here: 85.5 us
  Pallas kernels  76 us (89%)
  other arithmetic  6.35 us (7%)
  local copies, waits for them, and re-layouts  2.4 us (3%)
    pallas_call x1, Pallas kernels, body(): pl.pallas_call(functools.partial(kernel, (n_clus, n_trip, n_mode, modes,...  76 us
    concatenate x1, other arithmetic, body(): jnp.concatenate([jnp.pad(force_third, ((0, 0), (0, 0), (0, npad - flat)))...  5.46 us

commit v1 on v0

v1 whole, which is shorter than its diff:
```python
import functools

import jax
import jax.numpy as jnp
from jax import lax
from jax.experimental import pallas as pl
from jax.experimental.pallas import tpu as pltpu
from jax.sharding import PartitionSpec as P

smearing = 0.3
MESH = pl.DeviceIdType.MESH
LANES = 128
f32 = jnp.float32
bf16 = jnp.bfloat16


def up(value, step):
    return -(-value // step) * step


def pick(index, options):
    chosen = options[0]
    for position in range(1, len(options)):
        chosen = jnp.where(index == position, options[position], chosen)
    return chosen


def kernel(
    dims,
    force_ref,
    tail_ref,
    eig_ref,
    send_rows_ref,
    table_ref,
    irr_ref,
    mult_ref,
    drive_ref,
    bound_ref,
    gamma_ref,
    dev_ref,
    blocks,
    tails,
    wbuf,
    left,
    asked,
    wanted,
    outgoing,
    arrived,
    mine,
    other,
    zbuf,
    tre,
    tim,
    w0buf,
    ratebuf,
    coupbuf,
    msg,
    inbox,
    f_send,
    f_recv,
    t_send,
    t_recv,
    c_send,
    c_recv,
    e_send,
    e_recv,
    p_send,
    p_recv,
    m_send,
    m_recv,
):
    n_clus, n_trip, n_mode, modes, half, rp, cl, slot, wide = dims
    ep = eig_ref.shape[1]
    flat = force_ref.shape[2]
    unit_rows = cl * rp
    chunks = zbuf.shape[1] // wide
    me_c = lax.axis_index("clus")
    me_t = lax.axis_index("trip")
    me_m = lax.axis_index("mode")
    sib = (me_c, me_t, 1 - me_m)
    odd = lax.rem(me_t, 2)
    low, high = lax.rem(me_c, 2), me_c // 2
    near = (me_c + (1 - odd) * (1 - 2 * low) + odd * (2 - 4 * high), me_t, me_m)
    far = (me_c + odd * (1 - 2 * low) + (1 - odd) * (2 - 4 * high), me_t, me_m)
    plane = (me_c, me_t + 1 - 2 * odd, me_m)

    peers = []
    for dt in range(n_trip):
        for dc in range(n_clus):
            if dt or dc:
                peers.append((dt, dc))

    def peer_id(dt, dc):
        return (lax.rem(me_c + dc, n_clus), lax.rem(me_t + dt, n_trip), me_m)

    barrier = pltpu.get_barrier_semaphore()
    for dt, dc in peers:
        pl.semaphore_signal(barrier, inc=1, device_id=peer_id(dt, dc), device_id_type=MESH)
    pl.semaphore_signal(barrier, inc=1, device_id=sib, device_id_type=MESH)

    asked[...] = jnp.zeros_like(asked)
    for j in range(3):
        asked[j : j + 1, :] = jnp.full((1, LANES), table_ref[me_c, j].astype(f32))

    whole = half // 16 * 16
    for n in range(chunks):
        lo = n * wide
        hi = min(lo + wide, flat)
        for r in range(cl):
            at = r * rp
            if hi < lo + wide:
                edge = hi // LANES * LANES
                blocks[at : at + rp, edge : lo + wide] = jnp.zeros((rp, lo + wide - edge), bf16)
            blocks[at : at + whole, lo:hi] = force_ref[r, :whole, lo:hi]
            rest = force_ref[r, whole:, lo:hi].astype(f32)
            under = jnp.zeros((rp - half, hi - lo), f32)
            blocks[at + whole : at + rp, lo:hi] = jnp.concatenate([rest, under], axis=0).astype(bf16)

    pl.semaphore_wait(barrier, len(peers) + 1)

    def unit(k, m, n):
        return blocks.at[pl.ds((k * 2 + m) * unit_rows, unit_rows), pl.ds(n * wide, wide)]

    started = []

    def copy_of(src, k, m, n, device):
        return pltpu.make_async_remote_copy(
            src_ref=src,
            dst_ref=unit(k, m, n),
            send_sem=f_send.at[k, m, n],
            recv_sem=f_recv.at[k, m, n],
            device_id=device,
            device_id_type=MESH,
        )

    def send(src, k, m, n, device):
        copy = copy_of(src, k, m, n, device)
        copy.start()
        started.append(copy)

    def got(k, m, n):
        copy_of(unit(k, m, n), k, m, n, sib).wait_recv()

    asks = []
    for dt in range(1, n_trip):
        copy = pltpu.make_async_remote_copy(
            src_ref=asked,
            dst_ref=wanted.at[dt],
            send_sem=t_send.at[dt],
            recv_sem=t_recv.at[dt],
            device_id=(me_c, lax.rem(me_t + dt, n_trip), me_m),
            device_id_type=MESH,
        )
        copy.start()
        asks.append(copy)
    phase_copies = []
    for k, device in ((1, near), (2, far), (3, (3 - me_c, me_t, me_m))):
        copy = pltpu.make_async_remote_copy(
            src_ref=tail_ref,
            dst_ref=tails.at[k],
            send_sem=c_send.at[k],
            recv_sem=c_recv.at[k],
            device_id=device,
            device_id_type=MESH,
        )
        copy.start()
        phase_copies.append(copy)
    for n in range(chunks):
        send(unit(0, 0, n), 1, 0, n, near)
    for n in range(chunks):
        send(unit(0, 0, n), 0, 1, n, sib)

    def answer(dt, wishes):
        target = lax.rem(me_t - dt + n_trip, n_trip)
        for j in range(3):
            wish = wishes[j : j + 1, :]
            block = jnp.zeros((ep, LANES), f32)
            for k in range(slot):
                row = send_rows_ref[0, target * slot + k]
                name = (me_t * slot + k).astype(f32)
                block = jnp.where(wish == name, eig_ref[row].astype(f32), block)
            outgoing[dt, j] = block.astype(bf16)

    answer(0, asked[...])
    eig_copies = []
    for dt in range(1, n_trip):
        asks[dt - 1].wait()
        answer(dt, wanted[dt])
    for dt in range(1, n_trip):
        copy = pltpu.make_async_remote_copy(
            src_ref=outgoing.at[dt],
            dst_ref=arrived.at[dt],
            send_sem=e_send.at[dt],
            recv_sem=e_recv.at[dt],
            device_id=(me_c, lax.rem(me_t - dt + n_trip, n_trip), me_m),
            device_id_type=MESH,
        )
        copy.start()
        eig_copies.append(copy)
    arrived[0] = outgoing[0]

    def direct(n):
        got(1, 0, n)
        send(unit(1, 0, n), 2, 0, n, plane)
        send(unit(1, 0, n), 3, 0, n, far)
        send(unit(1, 0, n), 1, 1, n, sib)

    def second(n):
        got(2, 0, n)
        send(unit(2, 0, n), 2, 1, n, sib)
        got(3, 0, n)
        send(unit(3, 0, n), 3, 1, n, sib)

    direct(0)
    for copy in eig_copies:
        copy.wait()
    for j in range(3):
        source = table_ref[me_c, j] // slot
        mine[j] = arrived[lax.rem(source - me_t + n_trip, n_trip), j]
    pair = pltpu.make_async_remote_copy(
        src_ref=mine,
        dst_ref=other,
        send_sem=p_send,
        recv_sem=p_recv,
        device_id=sib,
        device_id_type=MESH,
    )
    pair.start()
    direct(1)
    pair.wait()

    first = me_m == 0

    def complex_of(j):
        a = mine[j].astype(f32)
        b = other[j].astype(f32)
        return jnp.where(first, a, b), jnp.where(first, b, a)

    re0, im0 = complex_of(0)
    re1, im1 = complex_of(1)
    re2, im2 = complex_of(2)
    f0 = re0[modes : modes + 1]
    f1, d1 = re1[modes : modes + 1], im1[modes : modes + 1]
    f2, d2 = re2[modes : modes + 1], im2[modes : modes + 1]

    def half_rows(mat):
        return pick(me_m, [mat[m * half : m * half + rp] for m in range(n_mode)])

    fill = jnp.zeros((rp - half, LANES), f32)

    def lead(mat, m):
        part = mat[m * half : (m + 1) * half]
        stacked = jnp.concatenate([part, fill] * cl, axis=0)
        return half_rows(jnp.transpose(stacked))

    lead_re = [lead(re0, m) for m in range(n_mode)]
    lead_im = [lead(im0, m) for m in range(n_mode)]
    lane_k = lax.broadcasted_iota(jnp.int32, (rp, cl * rp), 1)
    lane = lax.broadcasted_iota(jnp.int32, (1, LANES), 1)

    def weights(k):
        cosines, sines = [], []
        for r in range(cl):
            tail = tail_ref[r] if k == 0 else tails[k, r]
            cosines.append(jnp.sum(jnp.where(lane == me_c, tail[0:1], 0.0), axis=1, keepdims=True))
            sines.append(jnp.sum(jnp.where(lane == me_c, tail[1:2], 0.0), axis=1, keepdims=True))
        cosv, sinv = cosines[0], sines[0]
        for r in range(1, cl):
            cosv = jnp.where(lane_k >= r * rp, cosines[r], cosv)
            sinv = jnp.where(lane_k >= r * rp, sines[r], sinv)
        for m in range(2):
            wre = jnp.where(first, lead_re[m], lead_re[1 - m])
            wim = jnp.where(first, lead_im[m], lead_im[1 - m])
            at = (k * 2 + m) * unit_rows
            wbuf[:, at : at + unit_rows] = jnp.concatenate(
                [cosv * wre - sinv * wim, cosv * wim + sinv * wre], axis=0
            ).astype(bf16)

    e2a = jnp.concatenate([re2, im2], axis=1)[:modes].astype(bf16)
    e2b = jnp.concatenate([-im2, re2], axis=1)[:modes].astype(bf16)
    row_id = lax.broadcasted_iota(jnp.int32, (ep, LANES), 0)
    e1re_t = jnp.transpose(jnp.where(row_id < modes, re1, 0.0))[:ep]
    e1im_t = jnp.transpose(jnp.where(row_id < modes, im1, 0.0))[:ep]
    left[:, :ep] = jnp.concatenate([e1re_t, e1im_t], axis=0).astype(bf16)
    left[:, ep:] = jnp.concatenate([-e1im_t, e1re_t], axis=0).astype(bf16)

    def column(row):
        return jnp.transpose(jnp.broadcast_to(row, (LANES, LANES)))

    w0buf[...] = half_rows(column(f0))
    w1 = jnp.where(row_id < modes, column(f1)[:ep], 1.0)
    w2 = jnp.where(lane < modes, f2, 1.0)
    occ = jnp.where(row_id < modes, column(d1)[:ep], 0.0) + jnp.where(lane < modes, d2, 0.0)
    inverse = 1.0 / (w1 * w2)
    tre[modes * rp :, :] = jnp.zeros(((ep - modes) * rp, LANES), f32)
    tim[modes * rp :, :] = jnp.zeros(((ep - modes) * rp, LANES), f32)

    def contract(n):
        for k in range(4):
            got(k, 1, n)
        step = wide // 2
        for i in range(2):
            cols = slice(n * wide + i * step, n * wide + (i + 1) * step)
            zbuf[:, cols] = jnp.dot(wbuf[...], blocks[:, cols], preferred_element_type=f32)
        for b in range(modes):
            if not n * wide < (b + 1) * modes <= (n + 1) * wide:
                continue
            part = zbuf[:, b * modes : (b + 1) * modes].astype(bf16)
            out = jnp.dot(part[:rp], e2a, preferred_element_type=f32) + jnp.dot(
                part[rp:], e2b, preferred_element_type=f32
            )
            tre[b * rp : (b + 1) * rp, :] = out[:, :LANES]
            tim[b * rp : (b + 1) * rp, :] = out[:, LANES:]

    for copy in phase_copies:
        copy.wait()
    for k in range(4):
        weights(k)

    for n in range(2, chunks + 3):
        if n < chunks:
            direct(n)
        if 0 <= n - 2 < chunks:
            second(n - 2)
        if 0 <= n - 3 < chunks:
            contract(n - 3)

    scaled = 0.5 / (smearing * smearing)
    ratebuf[...] = jnp.zeros_like(ratebuf)
    coupbuf[...] = jnp.zeros_like(coupbuf)

    def modes_step(p, carry):
        def rows(ref):
            return jnp.concatenate(
                [ref[pl.ds(2 * p + i, ep, stride=rp), :] for i in range(2)], axis=1
            ).astype(bf16)

        both = jnp.concatenate([rows(tre), rows(tim)], axis=0)
        amp = jnp.dot(left[...], both, preferred_element_type=f32)
        square = amp * amp
        square = square[:ep] + square[ep:]
        for i in range(2):
            w0 = w0buf[pl.ds(2 * p + i, 1), :]
            decays = w0 - w1 - w2
            merges = w0 + w1 - w2
            gauss = jnp.exp(-scaled * decays * decays) + jnp.exp(-scaled * merges * merges)
            value = square[:, i * LANES : (i + 1) * LANES] * gauss * inverse
            ratebuf[pl.ds(2 * p + i, 1), :] = jnp.sum(value, axis=0, keepdims=True)
            coupbuf[pl.ds(2 * p + i, 1), :] = jnp.sum(value * occ, axis=0, keepdims=True)
        return carry

    lax.fori_loop(0, up(half, 2) // 2, modes_step, 0)

    factor = mult_ref[me_c].astype(f32)
    w0_row = pick(me_m, [f0[:, m * half : (m + 1) * half] for m in range(n_mode)])
    rate = jnp.sum(jnp.transpose(ratebuf[...]), axis=0, keepdims=True)[:, :half] / w0_row * factor
    coup = jnp.sum(jnp.transpose(coupbuf[...]), axis=0, keepdims=True)[:, :half] / w0_row * factor
    msg[...] = jnp.zeros_like(msg)
    msg[0:1, 0:half] = rate
    msg[1:2, 0:half] = coup
    msg[2:3, :] = jnp.full((1, LANES), irr_ref[me_c].astype(f32))

    copies = []
    for index, (dt, dc) in enumerate(peers):
        copy = pltpu.make_async_remote_copy(
            src_ref=msg,
            dst_ref=inbox.at[index],
            send_sem=m_send.at[index],
            recv_sem=m_recv.at[index],
            device_id=peer_id(dt, dc),
            device_id_type=MESH,
        )
        copy.start()
        copies.append(copy)
    for copy in started:
        copy.wait_send()
    for copy in copies:
        copy.wait()

    nq = gamma_ref.shape[0]
    for q in range(nq):
        name = (me_t * nq + q).astype(f32)

        def kept(tile):
            return jnp.where(tile[2:3, :half] == name, tile[0:2, :half], 0.0)

        total = kept(msg[...])
        if len(peers) <= 16:
            for index in range(len(peers)):
                total = total + kept(inbox[index])
        else:
            total = lax.fori_loop(0, len(peers), lambda i, acc: acc + kept(inbox[i]), total)
        gamma = total[0:1] + bound_ref[q : q + 1, :]
        gamma_ref[q : q + 1, :] = gamma
        dev_ref[q : q + 1, :] = (drive_ref[q : q + 1, :] + total[1:2]) / gamma


def body(
    force_third,
    phase_angle,
    eigenvectors,
    frequencies,
    deviation,
    send_rows,
    trip_table,
    irreducible,
    multiplicity,
    drive_term,
    boundary,
):
    n_clus, n_trip, n_mode = (lax.axis_size(name) for name in ("clus", "trip", "mode"))
    cl, half, flat = force_third.shape
    points, modes, _ = eigenvectors.shape
    slot = send_rows.shape[1] // n_trip
    wide = 1024
    rp = up(half, 16)
    ep = up(modes + 1, 16)
    npad = up(flat, wide)
    chunks = npad // wide
    angles = phase_angle.astype(f32)
    trig = jnp.stack([jnp.cos(angles), jnp.sin(angles)], axis=1).astype(bf16).astype(f32)
    tail = jnp.pad(trig, ((0, 0), (0, 6), (0, LANES - trig.shape[2])))
    first = lax.axis_index("mode") == 0
    part = jnp.where(first, eigenvectors[..., :modes], eigenvectors[..., modes:])
    extra = jnp.where(first, frequencies, deviation)[:, None]
    eig = jnp.pad(
        jnp.concatenate([part, extra], axis=1),
        ((0, 0), (0, ep - modes - 1), (0, LANES - modes)),
    )
    n_peers = n_clus * n_trip - 1
    vmem = pl.BlockSpec(memory_space=pltpu.VMEM)
    smem = pl.BlockSpec(memory_space=pltpu.SMEM)
    out = jax.ShapeDtypeStruct(boundary.shape, f32)
    dma = pltpu.SemaphoreType.DMA
    return tuple(
        pl.pallas_call(
            functools.partial(
                kernel, (n_clus, n_trip, n_mode, modes, half, rp, cl, slot, wide)
            ),
            out_shape=(out, out),
            in_specs=[vmem, vmem, vmem, smem, smem, smem, smem, vmem, vmem],
            out_specs=(vmem, vmem),
            scratch_shapes=[
                pltpu.VMEM((n_clus * n_mode * cl * rp, npad), bf16),
                pltpu.VMEM((n_clus, cl, 8, LANES), f32),
                pltpu.VMEM((2 * rp, n_clus * n_mode * cl * rp), bf16),
                pltpu.VMEM((2 * ep, 2 * ep), bf16),
                pltpu.VMEM((8, LANES), f32),
                pltpu.VMEM((n_trip, 8, LANES), f32),
                pltpu.VMEM((n_trip, 3, ep, LANES), bf16),
                pltpu.VMEM((n_trip, 3, ep, LANES), bf16),
                pltpu.VMEM((3, ep, LANES), bf16),
                pltpu.VMEM((3, ep, LANES), bf16),
                pltpu.VMEM((2 * rp, npad), f32),
                pltpu.VMEM((ep * rp, LANES), f32),
                pltpu.VMEM((ep * rp, LANES), f32),
                pltpu.VMEM((rp, LANES), f32),
                pltpu.VMEM((LANES, LANES), f32),
                pltpu.VMEM((LANES, LANES), f32),
                pltpu.VMEM((8, LANES), f32),
                pltpu.VMEM((n_peers, 8, LANES), f32),
                dma((n_clus, n_mode, chunks)),
                dma((n_clus, n_mode, chunks)),
                dma((n_trip,)),
                dma((n_trip,)),
                dma((n_clus,)),
                dma((n_clus,)),
                dma((n_trip,)),
                dma((n_trip,)),
                dma,
                dma,
                dma((n_peers,)),
                dma((n_peers,)),
            ],
            compiler_params=pltpu.CompilerParams(
                collective_id=0, has_side_effects=True, vmem_limit_bytes=48 * 1024 * 1024
            ),
        )(force_third, tail, eig, send_rows, trip_table, irreducible, multiplicity, drive_term, boundary)
    )


def solution(mesh):
    return jax.shard_map(
        body,
        mesh=mesh,
        in_specs=(
            P("clus", "mode", None),
            P("clus", "trip"),
            P("trip", None, None),
            P("trip", None),
            P("trip", None),
            P("trip", None),
            P("trip", None),
            P("trip"),
            P("trip"),
            P("trip", "mode"),
            P("trip", "mode"),
        ),
        out_specs=(P("trip", "mode"), P("trip", "mode")),
        check_vma=False,
    )
```

time: 85.8 us -> 68 us (0.79)
  Pallas kernels: 76 us -> 62.3 us
  other arithmetic: 6.35 us -> 1.65 us
    pallas_call x1, Pallas kernels: 76 us -> 62.3 us  [body(): pl.pallas_call(functools.partial(kernel, (n_clus, n_trip, n_mode, modes,...]
    concatenate x1 -> x0, other arithmetic: 5.46 us -> none  [body(): jnp.concatenate([jnp.pad(force_third, ((0, 0), (0, 0), (0, npad - flat)))...]
    slice x1, local copies, waits for them, and re-layouts: 0.12 us -> 1.21 us  [body(): eigenvectors[..., :modes]]
    concatenate x1 -> x0, local copies, waits for them, and re-layouts: 0.87 us -> none  [body(): jnp.concatenate([jnp.pad(force_third, ((0, 0), (0, 0), (0, npad - flat)))...]
    unnamed x20 -> x17, local copies, waits for them, and re-layouts: 1.41 us -> 1.89 us
where the time goes in v1:
time: 68 us; the launch traced here: 67.8 us
  Pallas kernels  62.3 us (92%)
  local copies, waits for them, and re-layouts  3.11 us (5%)
  other arithmetic  1.65 us (2%)
  between operations  0.8 us (1%)
    pallas_call x1, Pallas kernels, body(): pl.pallas_call(functools.partial(kernel, (n_clus, n_trip, n_mode, modes,...  62.3 us
    unnamed x17, local copies, waits for them, and re-layouts  1.89 us

profile of v1, /device:TPU:0, one launch (start us, length us, event | category | flops | bytes accessed | tf_op | source)
XLA Modules:
  0.0 67.8 jit_solution(12613490009352368709)
XLA Ops:
  0.6 0.0 copy-start.6
  0.6 0.8 %fusion.16 = (bf16[2,1,4]{2,0,1:T(2,128)(2,1)S(1)}, bf16[2,1,4]{2,0,1:T(2,128)(2,1)S(1)}) fusion(bf16[2,4]{1,0:T(2,128)(2,1)} %param.12), kind=kLoop, calls=%fused_computation.24 | loop fusion | flops 24 | bytes 48 | tf_op jit(solution)/shard_map/stack | solution.py:421
  1.5 0.7 %select_bitcast_fusion = bf16[8,1,90]{2,0,1:T(8,128)(2,1)S(1)} fusion(bf16[8,90]{1,0:T(8,128)(2,1)} %param.14, bf16[8,90]{1,0:T(8,128)(2,1)} %param.15, pred[]{:T(512)S(6)} %eq.3), kind=kLoop, calls=%fused_computation.18 | loop fusion | flops 720 | bytes 4321 | tf_op jit(solution)/shard_map/broadcast_in_dim | solution.py:425
  2.2 1.2 %fusion.17 = (bf16[8,90,90]{2,0,1:T(8,128)(2,1)S(1)}, bf16[8,90,90]{2,0,1:T(8,128)(2,1)S(1)}) fusion(bf16[8,90,180]{2,0,1:T(8,128)(2,1)} %param.13), kind=kLoop, calls=%fused_computation.25 | loop fusion | bytes 518400 | tf_op jit(solution)/shard_map/slice | solution.py:424
  3.4 0.1 copy_select_fusion
  3.5 0.1 fusion.5.eig_ref
  3.6 0.0 copy-done.6
  3.6 0.0 copy-start
  3.6 0.0 copy-start.1
  3.6 0.0 copy-start.2
  3.6 0.0 copy-start.3
  3.6 0.0 copy-start.4
  3.6 0.0 copy-start.5
  3.6 0.8 %copy.23.force_ref = bf16[2,45,8100]{2,1,0:T(8,128)(2,1)S(1)} copy(bf16[2,45,8100]{2,0,1:T(2,128)(2,1)S(1)} %copy-done.6) | data formatting | bytes 2916000 | tf_op args[0]
  4.5 0.0 copy-done
  4.5 0.0 copy-done.1
  4.5 0.0 copy-done.2
  4.5 0.0 copy-done.3
  4.5 0.0 copy-done.4
  4.5 0.0 copy-done.5
  4.5 62.3 %shard_map.122 = (f32[1,45]{1,0:T(1,128)S(1)}, f32[1,45]{1,0:T(1,128)S(1)}) custom-call(bf16[2,45,8100]{2,1,0:T(8,128)(2,1)S(1)} %copy.23.force_ref, f32[2,8,128]{2,1,0:T(8,128)S(1)} %fusion.12.tail_ref, bf16[8,96,128]{2,1,0:T(8,128)(2,1)S(1)} %fusion.5.eig_ref, s32[1,32]{1,0:T(1,128)S(1)} %copy-done.1, s32[4,3]{1,0:T(4,128)S(1)} %copy-done, ...), custom_call_target="tpu_custom_call" | custom-call | tf_op jit(solution)/shard_map/pallas_call | solution.py:436
  66.8 0.5 copy.30
  67.3 0.5 copy.31
  (4 shorter events, 0.0 us)
Async XLA Ops:
  0.6 2.9 %copy-start.6 = (bf16[2,45,8100]{2,0,1:T(2,128)(2,1)S(1)}, bf16[2,45,8100]{2,0,1:T(2,128)(2,1)}, u32[]{:S(2)}) copy-start(bf16[2,45,8100]{2,0,1:T(2,128)(2,1)} %param.11) | copy-start | bytes 4374004
  3.6 0.9 %copy-start = (s32[4,3]{1,0:T(4,128)S(1)}, s32[4,3]{1,0:T(4,128)}, u32[]{:S(2)}) copy-start(s32[4,3]{1,0:T(4,128)} %table_ref.1) | copy-start | bytes 148
  3.6 0.9 %copy-start.1 = (s32[1,32]{1,0:T(1,128)S(1)}, s32[1,32]{1,0:T(1,128)}, u32[]{:S(2)}) copy-start(s32[1,32]{1,0:T(1,128)} %send_rows_ref.1) | copy-start | bytes 388
  3.6 0.9 %copy-start.2 = (s32[4]{0:T(128)S(1)}, s32[4]{0:T(128)}, u32[]{:S(2)}) copy-start(s32[4]{0:T(128)} %irr_ref.1) | copy-start | bytes 52
  3.6 0.9 %copy-start.3 = (s32[4]{0:T(128)S(1)}, s32[4]{0:T(128)}, u32[]{:S(2)}) copy-start(s32[4]{0:T(128)} %mult_ref.1) | copy-start | bytes 52
  3.6 0.9 %copy-start.4 = (f32[1,45]{1,0:T(1,128)S(1)}, f32[1,45]{1,0:T(1,128)}, u32[]{:S(2)}) copy-start(f32[1,45]{1,0:T(1,128)} %drive_ref.1) | copy-start | bytes 544
  3.6 0.9 %copy-start.5 = (f32[1,45]{1,0:T(1,128)S(1)}, f32[1,45]{1,0:T(1,128)}, u32[]{:S(2)}) copy-start(f32[1,45]{1,0:T(1,128)} %bound_ref.1) | copy-start | bytes 544

commit v2 on v1

--- a/solution.py
+++ b/solution.py
@@ -298,10 +298,8 @@
     def contract(n):
         for k in range(4):
             got(k, 1, n)
-        step = wide // 2
-        for i in range(2):
-            cols = slice(n * wide + i * step, n * wide + (i + 1) * step)
-            zbuf[:, cols] = jnp.dot(wbuf[...], blocks[:, cols], preferred_element_type=f32)
+        cols = slice(n * wide, (n + 1) * wide)
+        zbuf[:, cols] = jnp.dot(wbuf[...], blocks[:, cols], preferred_element_type=f32)
         for b in range(modes):
             if not n * wide < (b + 1) * modes <= (n + 1) * wide:
                 continue
@@ -326,13 +324,13 @@
             contract(n - 3)
 
     scaled = 0.5 / (smearing * smearing)
-    ratebuf[...] = jnp.zeros_like(ratebuf)
-    coupbuf[...] = jnp.zeros_like(coupbuf)
-
-    def modes_step(p, carry):
+    lower = w1 + w2
+    upper = w1 - w2
+
+    def one_pair(s0):
         def rows(ref):
             return jnp.concatenate(
-                [ref[pl.ds(2 * p + i, ep, stride=rp), :] for i in range(2)], axis=1
+                [ref[pl.ds(s0 + i, ep, stride=rp), :] for i in range(2)], axis=1
             ).astype(bf16)
 
         both = jnp.concatenate([rows(tre), rows(tim)], axis=0)
@@ -340,21 +338,34 @@
         square = amp * amp
         square = square[:ep] + square[ep:]
         for i in range(2):
-            w0 = w0buf[pl.ds(2 * p + i, 1), :]
-            decays = w0 - w1 - w2
-            merges = w0 + w1 - w2
-            gauss = jnp.exp(-scaled * decays * decays) + jnp.exp(-scaled * merges * merges)
+            w0 = w0buf[pl.ds(s0 + i, 1), :]
+            decays = w0 - lower
+            merges = w0 + upper
+            gauss = jnp.exp(-scaled * (decays * decays)) + jnp.exp(-scaled * (merges * merges))
             value = square[:, i * LANES : (i + 1) * LANES] * gauss * inverse
-            ratebuf[pl.ds(2 * p + i, 1), :] = jnp.sum(value, axis=0, keepdims=True)
-            coupbuf[pl.ds(2 * p + i, 1), :] = jnp.sum(value * occ, axis=0, keepdims=True)
+            at = pl.ds(pl.multiple_of((s0 + i) * 8, 8), 8)
+            ratebuf[at, :] = jnp.sum(value.reshape(ep // 8, 8, LANES), axis=0)
+            coupbuf[at, :] = jnp.sum((value * occ).reshape(ep // 8, 8, LANES), axis=0)
+
+    group = 4
+
+    def modes_step(p, carry):
+        for i in range(group):
+            one_pair((p * group + i) * 2)
         return carry
 
-    lax.fori_loop(0, up(half, 2) // 2, modes_step, 0)
+    lax.fori_loop(0, rp // (2 * group), modes_step, 0)
+
+    def folded(ref):
+        total = ref[pl.ds(0, rp, stride=8), :]
+        for i in range(1, 8):
+            total = total + ref[pl.ds(i, rp, stride=8), :]
+        return jnp.sum(jnp.transpose(total), axis=0, keepdims=True)[:, :half]
 
     factor = mult_ref[me_c].astype(f32)
     w0_row = pick(me_m, [f0[:, m * half : (m + 1) * half] for m in range(n_mode)])
-    rate = jnp.sum(jnp.transpose(ratebuf[...]), axis=0, keepdims=True)[:, :half] / w0_row * factor
-    coup = jnp.sum(jnp.transpose(coupbuf[...]), axis=0, keepdims=True)[:, :half] / w0_row * factor
+    rate = folded(ratebuf) / w0_row * factor
+    coup = folded(coupbuf) / w0_row * factor
     msg[...] = jnp.zeros_like(msg)
     msg[0:1, 0:half] = rate
     msg[1:2, 0:half] = coup
@@ -412,7 +423,7 @@
     cl, half, flat = force_third.shape
     points, modes, _ = eigenvectors.shape
     slot = send_rows.shape[1] // n_trip
-    wide = 1024
+    wide = 512
     rp = up(half, 16)
     ep = up(modes + 1, 16)
     npad = up(flat, wide)
@@ -455,8 +466,8 @@
                 pltpu.VMEM((ep * rp, LANES), f32),
                 pltpu.VMEM((ep * rp, LANES), f32),
                 pltpu.VMEM((rp, LANES), f32),
-                pltpu.VMEM((LANES, LANES), f32),
-                pltpu.VMEM((LANES, LANES), f32),
+                pltpu.VMEM((rp * 8, LANES), f32),
+                pltpu.VMEM((rp * 8, LANES), f32),
                 pltpu.VMEM((8, LANES), f32),
                 pltpu.VMEM((n_peers, 8, LANES), f32),
                 dma((n_clus, n_mode, chunks)),

time: 68 us -> 68.4 us (level)
  no operation moved by 1% of the time
where the time goes in v2:
time: 68.4 us; the launch traced here: 68.2 us
  Pallas kernels  62.6 us (92%)
  local copies, waits for them, and re-layouts  3.11 us (5%)
  other arithmetic  1.65 us (2%)
  between operations  0.8 us (1%)
    pallas_call x1, Pallas kernels, body(): pl.pallas_call(functools.partial(kernel, (n_clus, n_trip, n_mode, modes,...  62.6 us
    unnamed x17, local copies, waits for them, and re-layouts  1.89 us

profile of v2, /device:TPU:0, one launch (start us, length us, event | category | flops | bytes accessed | tf_op | source)
XLA Modules:
  0.0 68.2 jit_solution(13491616408034084854)
XLA Ops:
  0.6 0.0 copy-start.6
  0.6 0.8 %fusion.16 = (bf16[2,1,4]{2,0,1:T(2,128)(2,1)S(1)}, bf16[2,1,4]{2,0,1:T(2,128)(2,1)S(1)}) fusion(bf16[2,4]{1,0:T(2,128)(2,1)} %param.12), kind=kLoop, calls=%fused_computation.24 | loop fusion | flops 24 | bytes 48 | tf_op jit(solution)/shard_map/stack | solution.py:432
  1.5 0.7 %select_bitcast_fusion = bf16[8,1,90]{2,0,1:T(8,128)(2,1)S(1)} fusion(bf16[8,90]{1,0:T(8,128)(2,1)} %param.14, bf16[8,90]{1,0:T(8,128)(2,1)} %param.15, pred[]{:T(512)S(6)} %eq.3), kind=kLoop, calls=%fused_computation.18 | loop fusion | flops 720 | bytes 4321 | tf_op jit(solution)/shard_map/broadcast_in_dim | solution.py:436
  2.2 1.2 %fusion.17 = (bf16[8,90,90]{2,0,1:T(8,128)(2,1)S(1)}, bf16[8,90,90]{2,0,1:T(8,128)(2,1)S(1)}) fusion(bf16[8,90,180]{2,0,1:T(8,128)(2,1)} %param.13), kind=kLoop, calls=%fused_computation.25 | loop fusion | bytes 518400 | tf_op jit(solution)/shard_map/slice | solution.py:435
  3.4 0.1 copy_select_fusion
  3.5 0.1 fusion.5.eig_ref
  3.6 0.0 copy-done.6
  3.6 0.0 copy-start
  3.6 0.0 copy-start.1
  3.6 0.0 copy-start.2
  3.6 0.0 copy-start.3
  3.6 0.0 copy-start.4
  3.6 0.0 copy-start.5
  3.6 0.8 %copy.23.force_ref = bf16[2,45,8100]{2,1,0:T(8,128)(2,1)S(1)} copy(bf16[2,45,8100]{2,0,1:T(2,128)(2,1)S(1)} %copy-done.6) | data formatting | bytes 2916000 | tf_op args[0]
  4.5 0.0 copy-done
  4.5 0.0 copy-done.1
  4.5 0.0 copy-done.2
  4.5 0.0 copy-done.3
  4.5 0.0 copy-done.4
  4.5 0.0 copy-done.5
  4.5 62.6 %shard_map.122 = (f32[1,45]{1,0:T(1,128)S(1)}, f32[1,45]{1,0:T(1,128)S(1)}) custom-call(bf16[2,45,8100]{2,1,0:T(8,128)(2,1)S(1)} %copy.23.force_ref, f32[2,8,128]{2,1,0:T(8,128)S(1)} %fusion.12.tail_ref, bf16[8,96,128]{2,1,0:T(8,128)(2,1)S(1)} %fusion.5.eig_ref, s32[1,32]{1,0:T(1,128)S(1)} %copy-done.1, s32[4,3]{1,0:T(4,128)S(1)} %copy-done, ...), custom_call_target="tpu_custom_call" | custom-call | tf_op jit(solution)/shard_map/pallas_call | solution.py:447
  67.2 0.5 copy.30
  67.7 0.5 copy.31
  (4 shorter events, 0.0 us)
Async XLA Ops:
  0.6 2.9 %copy-start.6 = (bf16[2,45,8100]{2,0,1:T(2,128)(2,1)S(1)}, bf16[2,45,8100]{2,0,1:T(2,128)(2,1)}, u32[]{:S(2)}) copy-start(bf16[2,45,8100]{2,0,1:T(2,128)(2,1)} %param.11) | copy-start | bytes 4374004
  3.6 0.9 %copy-start = (s32[4,3]{1,0:T(4,128)S(1)}, s32[4,3]{1,0:T(4,128)}, u32[]{:S(2)}) copy-start(s32[4,3]{1,0:T(4,128)} %table_ref.1) | copy-start | bytes 148
  3.6 0.9 %copy-start.1 = (s32[1,32]{1,0:T(1,128)S(1)}, s32[1,32]{1,0:T(1,128)}, u32[]{:S(2)}) copy-start(s32[1,32]{1,0:T(1,128)} %send_rows_ref.1) | copy-start | bytes 388
  3.6 0.9 %copy-start.2 = (s32[4]{0:T(128)S(1)}, s32[4]{0:T(128)}, u32[]{:S(2)}) copy-start(s32[4]{0:T(128)} %irr_ref.1) | copy-start | bytes 52
  3.6 0.9 %copy-start.3 = (s32[4]{0:T(128)S(1)}, s32[4]{0:T(128)}, u32[]{:S(2)}) copy-start(s32[4]{0:T(128)} %mult_ref.1) | copy-start | bytes 52
  3.6 0.9 %copy-start.4 = (f32[1,45]{1,0:T(1,128)S(1)}, f32[1,45]{1,0:T(1,128)}, u32[]{:S(2)}) copy-start(f32[1,45]{1,0:T(1,128)} %drive_ref.1) | copy-start | bytes 544
  3.6 0.9 %copy-start.5 = (f32[1,45]{1,0:T(1,128)S(1)}, f32[1,45]{1,0:T(1,128)}, u32[]{:S(2)}) copy-start(f32[1,45]{1,0:T(1,128)} %bound_ref.1) | copy-start | bytes 544

commit v3 on v2

--- a/solution.py
+++ b/solution.py
@@ -49,6 +49,8 @@
     mine,
     other,
     zbuf,
+    zout,
+    zin,
     tre,
     tim,
     w0buf,
@@ -119,14 +121,14 @@
     pl.semaphore_wait(barrier, len(peers) + 1)
 
     def unit(k, m, n):
-        return blocks.at[pl.ds((k * 2 + m) * unit_rows, unit_rows), pl.ds(n * wide, wide)]
+        return blocks.at[pl.ds(k * unit_rows, unit_rows), pl.ds(n * wide, wide)]
 
     started = []
 
     def copy_of(src, k, m, n, device):
         return pltpu.make_async_remote_copy(
             src_ref=src,
-            dst_ref=unit(k, m, n),
+            dst_ref=zin.at[:, pl.ds(n * wide, wide)] if m else unit(k, m, n),
             send_sem=f_send.at[k, m, n],
             recv_sem=f_recv.at[k, m, n],
             device_id=device,
@@ -139,7 +141,8 @@
         started.append(copy)
 
     def got(k, m, n):
-        copy_of(unit(k, m, n), k, m, n, sib).wait_recv()
+        src = zout.at[:, pl.ds(n * wide, wide)] if m else unit(k, m, n)
+        copy_of(src, k, m, n, sib).wait_recv()
 
     asks = []
     for dt in range(1, n_trip):
@@ -167,8 +170,6 @@
         phase_copies.append(copy)
     for n in range(chunks):
         send(unit(0, 0, n), 1, 0, n, near)
-    for n in range(chunks):
-        send(unit(0, 0, n), 0, 1, n, sib)
 
     def answer(dt, wishes):
         target = lax.rem(me_t - dt + n_trip, n_trip)
@@ -203,13 +204,10 @@
         got(1, 0, n)
         send(unit(1, 0, n), 2, 0, n, plane)
         send(unit(1, 0, n), 3, 0, n, far)
-        send(unit(1, 0, n), 1, 1, n, sib)
 
     def second(n):
         got(2, 0, n)
-        send(unit(2, 0, n), 2, 1, n, sib)
         got(3, 0, n)
-        send(unit(3, 0, n), 3, 1, n, sib)
 
     direct(0)
     for copy in eig_copies:
@@ -243,18 +241,18 @@
     f1, d1 = re1[modes : modes + 1], im1[modes : modes + 1]
     f2, d2 = re2[modes : modes + 1], im2[modes : modes + 1]
 
-    def half_rows(mat):
-        return pick(me_m, [mat[m * half : m * half + rp] for m in range(n_mode)])
+    def half_rows(mat, which):
+        return pick(which, [mat[m * half : m * half + rp] for m in range(n_mode)])
 
     fill = jnp.zeros((rp - half, LANES), f32)
 
-    def lead(mat, m):
-        part = mat[m * half : (m + 1) * half]
-        stacked = jnp.concatenate([part, fill] * cl, axis=0)
-        return half_rows(jnp.transpose(stacked))
-
-    lead_re = [lead(re0, m) for m in range(n_mode)]
-    lead_im = [lead(im0, m) for m in range(n_mode)]
+    def lead(mat):
+        part = pick(me_m, [mat[m * half : (m + 1) * half] for m in range(n_mode)])
+        turned = jnp.transpose(jnp.concatenate([part, fill] * cl, axis=0))
+        return half_rows(turned, me_m), half_rows(turned, 1 - me_m)
+
+    lead_re = lead(re0)
+    lead_im = lead(im0)
     lane_k = lax.broadcasted_iota(jnp.int32, (rp, cl * rp), 1)
     lane = lax.broadcasted_iota(jnp.int32, (1, LANES), 1)
 
@@ -268,11 +266,10 @@
         for r in range(1, cl):
             cosv = jnp.where(lane_k >= r * rp, cosines[r], cosv)
             sinv = jnp.where(lane_k >= r * rp, sines[r], sinv)
-        for m in range(2):
-            wre = jnp.where(first, lead_re[m], lead_re[1 - m])
-            wim = jnp.where(first, lead_im[m], lead_im[1 - m])
-            at = (k * 2 + m) * unit_rows
-            wbuf[:, at : at + unit_rows] = jnp.concatenate(
+        at = k * unit_rows
+        for h in range(2):
+            wre, wim = lead_re[h], lead_im[h]
+            wbuf[h * 2 * rp : (h + 1) * 2 * rp, at : at + unit_rows] = jnp.concatenate(
                 [cosv * wre - sinv * wim, cosv * wim + sinv * wre], axis=0
             ).astype(bf16)
 
@@ -287,7 +284,7 @@
     def column(row):
         return jnp.transpose(jnp.broadcast_to(row, (LANES, LANES)))
 
-    w0buf[...] = half_rows(column(f0))
+    w0buf[...] = half_rows(column(f0), me_m)
     w1 = jnp.where(row_id < modes, column(f1)[:ep], 1.0)
     w2 = jnp.where(lane < modes, f2, 1.0)
     occ = jnp.where(row_id < modes, column(d1)[:ep], 0.0) + jnp.where(lane < modes, d2, 0.0)
@@ -295,11 +292,17 @@
     tre[modes * rp :, :] = jnp.zeros(((ep - modes) * rp, LANES), f32)
     tim[modes * rp :, :] = jnp.zeros(((ep - modes) * rp, LANES), f32)
 
+    def share(n):
+        cols = slice(n * wide, (n + 1) * wide)
+        part = jnp.dot(wbuf[...], blocks[:, cols], preferred_element_type=f32)
+        zbuf[:, cols] = part[: 2 * rp]
+        zout[:, cols] = part[2 * rp :].astype(bf16)
+        send(zout.at[:, pl.ds(n * wide, wide)], 0, 1, n, sib)
+
     def contract(n):
-        for k in range(4):
-            got(k, 1, n)
+        got(0, 1, n)
         cols = slice(n * wide, (n + 1) * wide)
-        zbuf[:, cols] = jnp.dot(wbuf[...], blocks[:, cols], preferred_element_type=f32)
+        zbuf[:, cols] = zbuf[:, cols] + zin[:, cols].astype(f32)
         for b in range(modes):
             if not n * wide < (b + 1) * modes <= (n + 1) * wide:
                 continue
@@ -315,13 +318,15 @@
     for k in range(4):
         weights(k)
 
-    for n in range(2, chunks + 3):
+    for n in range(2, chunks + 4):
         if n < chunks:
             direct(n)
         if 0 <= n - 2 < chunks:
             second(n - 2)
         if 0 <= n - 3 < chunks:
-            contract(n - 3)
+            share(n - 3)
+        if 0 <= n - 4 < chunks:
+            contract(n - 4)
 
     scaled = 0.5 / (smearing * smearing)
     lower = w1 + w2
@@ -452,9 +457,9 @@
             in_specs=[vmem, vmem, vmem, smem, smem, smem, smem, vmem, vmem],
             out_specs=(vmem, vmem),
             scratch_shapes=[
-                pltpu.VMEM((n_clus * n_mode * cl * rp, npad), bf16),
+                pltpu.VMEM((n_clus * cl * rp, npad), bf16),
                 pltpu.VMEM((n_clus, cl, 8, LANES), f32),
-                pltpu.VMEM((2 * rp, n_clus * n_mode * cl * rp), bf16),
+                pltpu.VMEM((2 * n_mode * rp, n_clus * cl * rp), bf16),
                 pltpu.VMEM((2 * ep, 2 * ep), bf16),
                 pltpu.VMEM((8, LANES), f32),
                 pltpu.VMEM((n_trip, 8, LANES), f32),
@@ -463,6 +468,8 @@
                 pltpu.VMEM((3, ep, LANES), bf16),
                 pltpu.VMEM((3, ep, LANES), bf16),
                 pltpu.VMEM((2 * rp, npad), f32),
+                pltpu.VMEM((2 * rp, npad), bf16),
+                pltpu.VMEM((2 * rp, npad), bf16),
                 pltpu.VMEM((ep * rp, LANES), f32),
                 pltpu.VMEM((ep * rp, LANES), f32),
                 pltpu.VMEM((rp, LANES), f32),

time: 68.4 us -> 68.6 us (level)
  no operation moved by 1% of the time
where the time goes in v3:
time: 68.6 us; the launch traced here: 68.4 us
  Pallas kernels  62.9 us (92%)
  local copies, waits for them, and re-layouts  3.11 us (5%)
  other arithmetic  1.65 us (2%)
  between operations  0.8 us (1%)
    pallas_call x1, Pallas kernels, body(): pl.pallas_call(functools.partial(kernel, (n_clus, n_trip, n_mode, modes,...  62.9 us
    unnamed x17, local copies, waits for them, and re-layouts  1.89 us

profile of v3, /device:TPU:0, one launch (start us, length us, event | category | flops | bytes accessed | tf_op | source)
XLA Modules:
  0.0 68.4 jit_solution(3147079435071781817)
XLA Ops:
  0.6 0.0 copy-start.6
  0.6 0.8 %fusion.16 = (bf16[2,1,4]{2,0,1:T(2,128)(2,1)S(1)}, bf16[2,1,4]{2,0,1:T(2,128)(2,1)S(1)}) fusion(bf16[2,4]{1,0:T(2,128)(2,1)} %param.12), kind=kLoop, calls=%fused_computation.24 | loop fusion | flops 24 | bytes 48 | tf_op jit(solution)/shard_map/stack | solution.py:437
  1.5 0.7 %select_bitcast_fusion = bf16[8,1,90]{2,0,1:T(8,128)(2,1)S(1)} fusion(bf16[8,90]{1,0:T(8,128)(2,1)} %param.14, bf16[8,90]{1,0:T(8,128)(2,1)} %param.15, pred[]{:T(512)S(6)} %eq.3), kind=kLoop, calls=%fused_computation.18 | loop fusion | flops 720 | bytes 4321 | tf_op jit(solution)/shard_map/broadcast_in_dim | solution.py:441
  2.2 1.2 %fusion.17 = (bf16[8,90,90]{2,0,1:T(8,128)(2,1)S(1)}, bf16[8,90,90]{2,0,1:T(8,128)(2,1)S(1)}) fusion(bf16[8,90,180]{2,0,1:T(8,128)(2,1)} %param.13), kind=kLoop, calls=%fused_computation.25 | loop fusion | bytes 518400 | tf_op jit(solution)/shard_map/slice | solution.py:440
  3.4 0.1 copy_select_fusion
  3.5 0.1 fusion.5.eig_ref
  3.6 0.0 copy-done.6
  3.6 0.0 copy-start
  3.6 0.0 copy-start.1
  3.6 0.0 copy-start.2
  3.6 0.0 copy-start.3
  3.6 0.0 copy-start.4
  3.6 0.0 copy-start.5
  3.6 0.8 %copy.23.force_ref = bf16[2,45,8100]{2,1,0:T(8,128)(2,1)S(1)} copy(bf16[2,45,8100]{2,0,1:T(2,128)(2,1)S(1)} %copy-done.6) | data formatting | bytes 2916000 | tf_op args[0]
  4.5 0.0 copy-done
  4.5 0.0 copy-done.1
  4.5 0.0 copy-done.2
  4.5 0.0 copy-done.3
  4.5 0.0 copy-done.4
  4.5 0.0 copy-done.5
  4.5 62.9 %shard_map.122 = (f32[1,45]{1,0:T(1,128)S(1)}, f32[1,45]{1,0:T(1,128)S(1)}) custom-call(bf16[2,45,8100]{2,1,0:T(8,128)(2,1)S(1)} %copy.23.force_ref, f32[2,8,128]{2,1,0:T(8,128)S(1)} %fusion.12.tail_ref, bf16[8,96,128]{2,1,0:T(8,128)(2,1)S(1)} %fusion.5.eig_ref, s32[1,32]{1,0:T(1,128)S(1)} %copy-done.1, s32[4,3]{1,0:T(4,128)S(1)} %copy-done, ...), custom_call_target="tpu_custom_call" | custom-call | tf_op jit(solution)/shard_map/pallas_call | solution.py:452
  67.4 0.5 copy.30
  67.9 0.5 copy.31
  (4 shorter events, 0.0 us)
Async XLA Ops:
  0.6 2.9 %copy-start.6 = (bf16[2,45,8100]{2,0,1:T(2,128)(2,1)S(1)}, bf16[2,45,8100]{2,0,1:T(2,128)(2,1)}, u32[]{:S(2)}) copy-start(bf16[2,45,8100]{2,0,1:T(2,128)(2,1)} %param.11) | copy-start | bytes 4374004
  3.6 0.9 %copy-start = (s32[4,3]{1,0:T(4,128)S(1)}, s32[4,3]{1,0:T(4,128)}, u32[]{:S(2)}) copy-start(s32[4,3]{1,0:T(4,128)} %table_ref.1) | copy-start | bytes 148
  3.6 0.9 %copy-start.1 = (s32[1,32]{1,0:T(1,128)S(1)}, s32[1,32]{1,0:T(1,128)}, u32[]{:S(2)}) copy-start(s32[1,32]{1,0:T(1,128)} %send_rows_ref.1) | copy-start | bytes 388
  3.6 0.9 %copy-start.2 = (s32[4]{0:T(128)S(1)}, s32[4]{0:T(128)}, u32[]{:S(2)}) copy-start(s32[4]{0:T(128)} %irr_ref.1) | copy-start | bytes 52
  3.6 0.9 %copy-start.3 = (s32[4]{0:T(128)S(1)}, s32[4]{0:T(128)}, u32[]{:S(2)}) copy-start(s32[4]{0:T(128)} %mult_ref.1) | copy-start | bytes 52
  3.6 0.9 %copy-start.4 = (f32[1,45]{1,0:T(1,128)S(1)}, f32[1,45]{1,0:T(1,128)}, u32[]{:S(2)}) copy-start(f32[1,45]{1,0:T(1,128)} %drive_ref.1) | copy-start | bytes 544
  3.6 0.9 %copy-start.5 = (f32[1,45]{1,0:T(1,128)S(1)}, f32[1,45]{1,0:T(1,128)}, u32[]{:S(2)}) copy-start(f32[1,45]{1,0:T(1,128)} %bound_ref.1) | copy-start | bytes 544
